TPU v7x, 32 devices: a whole 2x2x4 slice. The times are simulated.
32 devices in a mesh: dp: 4 (over y, x), token: 8 (over z, core).
Axes of the slice: x: 2, y: 2, z: 4, core: 2. Of those that a mesh axis runs over, the one named last changes fastest.
Arguments:
- mix_input: bfloat16 [1536, 8, 768], P('dp', 'token'), may hold values from -6 to 6
- out_grad: bfloat16 [1536, 8, 768], P('dp', 'token'), may hold values from -1.5 to 1.5
- w_up: bfloat16 [8, 768, 3072], P('token'), may hold values from -0.21875 to 0.21875
- w_down: bfloat16 [8, 3072, 768], P('token'), may hold values from -0.109375 to 0.109375
- gain_first: float32 [8, 768], P('token'), may hold values from 0.25 to 1.75
- gain_second: float32 [8, 768], P('token'), may hold values from 0.25 to 1.75
- owner_dev: int32 [8, 1536, 1], P('token', 'dp'), may hold values from 0 to 3; in each aligned block of 384 rows (0 to 383, 384 to 767, ..., all dimensions but the last counted through in order) at most 240 rows name the same one
- slot_row: int32 [8, 1536], P('token', 'dp'), may hold values from 0 to 255
Outputs:
- grad_up: float32 [8, 768, 3072], P('token', 'dp')
- grad_down: float32 [8, 3072, 768], P('token', 'dp')
- row_grad: float32 [8, 1024, 768], P('token', 'dp')
Inputs may be any that keep to these rules, and one draw needn't show every extreme that they name: `owner_dev`: in the rows of one device (aligned blocks of 384 samples of one token) no owner is named by more than 240 rows, a bound that some block reaches.
All inputs are finite; a program needn't handle non-finite values.
Results may differ from a plain program's by a relative error of at most 0.015.
Values may be sent and summed in bfloat16 or wider, within the bound.
A program may use at most 128 MiB of HBM per device.

v0:
```python
import jax
import jax.numpy as jnp
from jax import lax
from jax.sharding import PartitionSpec as P

HOT = 256
EPS = 1e-05
HALF_ROOT = 0.7071067811865476
INV_ROOT_TAU = 0.3989422804014327


def normalize(values):
    center = values - jnp.mean(values, axis=-1, keepdims=True)
    inv_scale = lax.rsqrt(jnp.mean(center * center, axis=-1, keepdims=True) + EPS)
    return (center * inv_scale, inv_scale)


def norm_back(grad_norm, normed, inv_scale):
    mean_grad = jnp.mean(grad_norm, axis=-1, keepdims=True)
    mean_proj = jnp.mean(grad_norm * normed, axis=-1, keepdims=True)
    return inv_scale * (grad_norm - mean_grad - normed * mean_proj)


def gelu_parts(pre_act):
    cumul = 0.5 * (1.0 + jax.scipy.special.erf(pre_act * HALF_ROOT))
    density = jnp.exp(-0.5 * pre_act * pre_act) * INV_ROOT_TAU
    return (pre_act * cumul, cumul + pre_act * density)


def contract_rows(left, right):
    return lax.dot_general(
        left, right, (((0,), (0,)), ((), ())), preferred_element_type=jnp.float32
    )


def contract_cols(left, right):
    return lax.dot_general(
        left, right, (((1,), (1,)), ((), ())), preferred_element_type=jnp.float32
    )


def per_device(mix_input, out_grad, w_up, w_down, gain_first, gain_second, owner_dev, slot_row):
    batch_rows = mix_input.shape[0]
    width = mix_input.shape[2]
    owners = lax.axis_size("dp")
    normed, inv_scale = normalize(mix_input[:, 0, :].astype(jnp.float32))
    hidden_in = (normed * gain_first[0]).astype(jnp.bfloat16)
    pre_act = jnp.dot(hidden_in, w_up[0], preferred_element_type=jnp.float32)
    act_value, act_slope = gelu_parts(pre_act)
    active = act_value.astype(jnp.bfloat16)
    outer_sum = jnp.dot(active, w_down[0], preferred_element_type=jnp.float32) + hidden_in.astype(
        jnp.float32
    )
    normed_out, inv_out = normalize(outer_sum)
    grad_wide = norm_back(
        out_grad[:, 0, :].astype(jnp.float32) * gain_second[0], normed_out, inv_out
    )
    grad_mid = grad_wide.astype(jnp.bfloat16)
    grad_act = contract_cols(grad_mid, w_down[0])
    grad_pre = (grad_act * act_slope).astype(jnp.bfloat16)
    up_whole = contract_rows(hidden_in, grad_pre)
    down_whole = contract_rows(active, grad_mid)
    grad_up, grad_down = (
        lax.psum_scatter(
            up_whole.astype(jnp.bfloat16), "dp", scatter_dimension=0, tiled=True
        ).astype(jnp.float32),
        lax.psum_scatter(
            down_whole.astype(jnp.bfloat16), "dp", scatter_dimension=0, tiled=True
        ).astype(jnp.float32),
    )
    grad_hidden = contract_cols(grad_pre, w_up[0]) + grad_wide
    grad_sum = norm_back(grad_hidden * gain_first[0], normed, inv_scale).astype(jnp.bfloat16)
    pieces = lax.axis_size("token")
    swapped = lax.all_to_all(
        grad_sum.reshape(batch_rows, pieces, width // pieces),
        "token",
        split_axis=1,
        concat_axis=1,
        tiled=True,
    )
    embed_grad = (
        grad_sum.astype(jnp.float32) + swapped.reshape(batch_rows, width).astype(jnp.float32)
    ).astype(jnp.bfloat16)
    owner_ids = owner_dev[0, :, 0]
    slot_ids = slot_row[0]
    capacity = max(2, 8 * (5 * batch_rows // (16 * owners)))
    owner_hot = (
        owner_ids[:, None] == lax.broadcasted_iota(jnp.int32, (batch_rows, owners), 1)
    ).astype(jnp.int32)
    rank_within = jnp.sum((jnp.cumsum(owner_hot, axis=0) - 1) * owner_hot, axis=1)
    place = owner_ids * capacity + rank_within
    dispatch_mask = (
        lax.broadcasted_iota(jnp.int32, (owners * capacity, batch_rows), 0) == place[None, :]
    )
    send_grad = jnp.dot(
        dispatch_mask.astype(jnp.bfloat16), embed_grad, preferred_element_type=jnp.float32
    )
    send_grad = send_grad.astype(jnp.bfloat16).reshape(owners, capacity, width)
    send_slot = jnp.sum(dispatch_mask.astype(jnp.int32) * (slot_ids + 1)[None, :], axis=1) - 1
    send_slot = send_slot.astype(jnp.float32).astype(jnp.bfloat16).reshape(owners, capacity)
    recv_grad, recv_slot = (
        lax.all_to_all(send_grad, "dp", split_axis=0, concat_axis=0, tiled=True),
        lax.all_to_all(send_slot, "dp", split_axis=0, concat_axis=0, tiled=True),
    )
    slot_values = recv_slot.reshape(1, owners * capacity).astype(jnp.float32)
    gather_hot = (
        lax.broadcasted_iota(jnp.int32, (HOT, owners * capacity), 0).astype(jnp.float32)
        == slot_values
    ).astype(jnp.bfloat16)
    row_grad = jnp.dot(
        gather_hot, recv_grad.reshape(owners * capacity, width), preferred_element_type=jnp.float32
    )
    return (grad_up[None], grad_down[None], row_grad[None])


def solution(mesh):
    placed = (
        P("dp", "token", None),
        P("dp", "token", None),
        P("token", None, None),
        P("token", None, None),
        P("token", None),
        P("token", None),
        P("token", "dp", None),
        P("token", "dp"),
    )
    return jax.shard_map(
        per_device,
        mesh=mesh,
        in_specs=placed,
        out_specs=(P("token", "dp", None), P("token", "dp", None), P("token", "dp", None)),
        check_vma=False,
    )
```

profile of v0, /device:TPU:0, one launch (start us, length us, event | category | flops | bytes accessed | tf_op | source)
XLA Modules:
  0.0 167.2 jit_solution(3373217656529832667)
XLA Ops:
  7.2 0.0 copy-start
  7.2 0.0 copy-start.2
  7.2 0.0 copy-start.3
  7.2 0.0 reduce-scatter.5.cloned.1.call-start
  7.2 1.3 convert_reduce_fusion
  8.5 1.4 fusion.36
  9.9 0.0 copy-done.2
  9.9 0.0 copy-done.3
  10.0 0.0 copy-done
  10.0 6.4 %multiply_convert_fusion = (bf16[384,3072]{1,0:T(8,128)(2,1)S(1)}, f32[384,3072]{1,0:T(8,128)}) fusion(bf16[1,768,3072]{2,1,0:T(8,128)(2,1)} %param.10, bf16[384,1,768]{2,0,1:T(8,128)(2,1)S(1)} %copy-done, f32[768]{0:T(1024)S(1)} %reduce.1, f32[384]{0:T(512)S(1)} %add_rsqrt_fusion.1, f32[384]{0:T(512)S(1)} %broadcast_multiply_fusion.5), kind=kOutput, calls=%fused_computation.17 | convolution fusion | flops 1819312128 | bytes 12392448 | tf_op jit(solution)/shard_map/dot_general | solution.py:48
  16.4 4.4 %fusion.64 = (f32[384]{0:T(512)S(1)}, f32[384,768]{1,0:T(8,128)S(1)}) fusion(f32[768]{0:T(1024)S(1)} %reduce.1, f32[384]{0:T(512)S(1)} %add_rsqrt_fusion.1, f32[384]{0:T(512)S(1)} %broadcast_multiply_fusion.5, bf16[384,1,768]{2,0,1:T(8,128)(2,1)S(1)} %copy-done, bf16[384,3072]{1,0:T(8,128)(2,1)S(1)} %get-tuple-element.7, bf16[1,3072,768]{2,1,0:T(8,128)(2,1)} %param.11), kind=kOutput, calls=%fused_computation.88 | convolution fusion | flops 1814298240 | bytes 8855040 | tf_op jit(solution)/shard_map/dot_general | solution.py:51
  20.8 0.0 copy-start.1
  20.8 0.3 multiply_reduce_fusion
  21.1 0.8 copy-done.1
  21.9 0.4 fusion.42
  22.3 4.7 %convolution_convert_fusion = bf16[3072,768]{1,0:T(8,128)(2,1)} fusion(bf16[384,3072]{1,0:T(8,128)(2,1)S(1)} %get-tuple-element.7, f32[384,768]{1,0:T(8,128)S(1)} %get-tuple-element.10, bf16[384,1,768]{2,0,1:T(8,128)(2,1)S(1)} %copy-done.1, f32[384]{0:T(512)S(1)} %get-tuple-element.12, f32[384]{0:T(512)S(1)} %get-tuple-element.13, f32[768]{0:T(1024)S(1)} %reduce.2, ...), kind=kOutput, calls=%fused_computation.1 | convolution fusion | flops 1816952832 | bytes 8856576 | tf_op jit(solution)/shard_map/dot_general | solution.py:31
  27.0 0.0 reduce-scatter.5.cloned.1.call-update
  27.0 0.0 reduce-scatter.3.cloned.1.call-start
  27.0 6.8 %fusion.5 = bf16[384,3072]{1,0:T(8,128)(2,1)S(1)} fusion(f32[384,3072]{1,0:T(8,128)} %get-tuple-element.8, bf16[1,3072,768]{2,1,0:T(8,128)(2,1)} %param.11, f32[384,768]{1,0:T(8,128)S(1)} %get-tuple-element.10, bf16[384,1,768]{2,0,1:T(8,128)(2,1)S(1)} %copy-done.1, f32[384]{0:T(512)S(1)} %get-tuple-element.12, f32[384]{0:T(512)S(1)} %get-tuple-element.13, ...), kind=kOutput, calls=%fused_computation.8 | convolution fusion | flops 1826390016 | bytes 13575168 | tf_op jit(solution)/shard_map/dot_general | solution.py:37
  33.9 0.0 copy-start.6
  33.9 1.4 copy-done.6
  35.3 4.7 %convolution_convert_fusion.1 = bf16[768,3072]{1,0:T(8,128)(2,1)} fusion(bf16[384,3072]{1,0:T(8,128)(2,1)S(1)} %fusion.5, bf16[384,1,768]{2,0,1:T(8,128)(2,1)S(1)} %copy-done, f32[768]{0:T(1024)S(1)} %reduce.1, f32[384]{0:T(512)S(1)} %add_rsqrt_fusion.1, f32[384]{0:T(512)S(1)} %broadcast_multiply_fusion.5), kind=kOutput, calls=%fused_computation.2 | convolution fusion | flops 1815773184 | bytes 7673856 | tf_op jit(solution)/shard_map/dot_general | solution.py:31
  40.0 0.0 reduce-scatter.3.cloned.1.call-update
  40.0 5.5 %fusion.63 = (f32[384]{0:T(512)S(1)}, f32[384]{0:T(512)S(1)}, f32[384,768]{1,0:T(8,128)S(1)}) fusion(f32[384]{0:T(512)S(1)} %add_rsqrt_fusion.1, f32[384]{0:T(512)S(1)} %broadcast_multiply_fusion.5, bf16[384,1,768]{2,0,1:T(8,128)(2,1)S(1)} %copy-done, f32[768]{0:T(1024)S(1)} %reduce.1, f32[384]{0:T(512)S(1)} %get-tuple-element.12, ...), kind=kOutput, calls=%fused_computation.87 | convolution fusion | flops 1816657152 | bytes 10635264 | tf_op jit(solution)/shard_map/dot_general | solution.py:37
  45.5 0.4 fusion.35
  45.9 0.0 copy-start.5
  45.9 0.0 copy-start.4
  45.9 1.1 copy.17
  47.0 6.6 %all-to-all-start.1 = ((bf16[384,8,96]{0,2,1:T(8,128)(2,1)}), bf16[384,8,96]{0,2,1:T(8,128)(2,1)S(1)}, u32[]{:S(2)}, u32[]{:S(2)}) async-start(bf16[384,8,96]{0,2,1:T(8,128)(2,1)} %bitcast.8), calls=%async_computation.3 | async-start | bytes 1179648 | tf_op jit(solution)/shard_map/all_to_all | solution.py:74
  53.6 0.0 copy-done.5
  53.7 1.2 reduce-window.6
  54.9 0.2 slice_reduce_fusion
  55.1 0.2 reduce-window.9
  55.3 0.0 copy-done.4
  55.3 0.1 add_bitcast_fusion
  55.4 0.2 select_reduce_fusion
  55.7 0.7 convert_element_type.137
  56.4 14.0 %all-to-all-done.1 = bf16[384,8,96]{0,2,1:T(8,128)(2,1)S(1)} async-done(((bf16[384,8,96]{0,2,1:T(8,128)(2,1)}), bf16[384,8,96]{0,2,1:T(8,128)(2,1)S(1)}, u32[]{:S(2)}, u32[]{:S(2)}) %all-to-all-start.1) | async-done | bytes 589856 | tf_op jit(solution)/shard_map/all_to_all | solution.py:74
  70.4 3.7 %all-to-all-start = ((bf16[4,1,240]{2,1,0:T(2,128)(2,1)}), bf16[4,1,240]{2,1,0:T(2,128)(2,1)S(1)}, u32[]{:S(2)}, u32[]{:S(2)}) async-start(bf16[4,1,240]{2,1,0:T(2,128)(2,1)} %convert_element_type.137), calls=%async_computation.2 | async-start | bytes 8192 | tf_op jit(solution)/shard_map/all_to_all | solution.py:103
  74.1 0.1 bitcast_convert_fusion.2
  74.2 0.4 copy.18
  74.6 2.1 %convolution_convert_fusion.2 = bf16[960,768]{1,0:T(8,128)(2,1)} fusion(s32[384]{0:T(512)S(1)} %multiply_add_fusion, f32[384,768]{1,0:T(8,128)S(1)} %copy.18, bf16[384,768]{1,0:T(8,128)(2,1)S(1)} %fusion.35), kind=kOutput, calls=%fused_computation.22 | convolution fusion | flops 568221696 | bytes 3245568 | tf_op jit(solution)/shard_map/dot_general | solution.py:95
  76.7 2.2 %all-to-all-done = bf16[4,1,240]{2,1,0:T(2,128)(2,1)S(1)} async-done(((bf16[4,1,240]{2,1,0:T(2,128)(2,1)}), bf16[4,1,240]{2,1,0:T(2,128)(2,1)S(1)}, u32[]{:S(2)}, u32[]{:S(2)}) %all-to-all-start) | async-done | bytes 1952 | tf_op jit(solution)/shard_map/all_to_all | solution.py:103
  78.9 3.6 %all-to-all-start.2 = ((bf16[4,240,768]{2,1,0:T(8,128)(2,1)}), bf16[4,240,768]{2,1,0:T(8,128)(2,1)S(1)}, u32[]{:S(2)}, u32[]{:S(2)}) async-start(bf16[4,240,768]{2,1,0:T(8,128)(2,1)} %bitcast.10), calls=%async_computation.4 | async-start | bytes 2949120 | tf_op jit(solution)/shard_map/all_to_all | solution.py:102
  82.5 0.1 reshape.147
  82.6 18.5 %all-to-all-done.2 = bf16[4,240,768]{2,1,0:T(8,128)(2,1)S(1)} async-done(((bf16[4,240,768]{2,1,0:T(8,128)(2,1)}), bf16[4,240,768]{2,1,0:T(8,128)(2,1)S(1)}, u32[]{:S(2)}, u32[]{:S(2)}) %all-to-all-start.2) | async-done | bytes 1474592 | tf_op jit(solution)/shard_map/all_to_all | solution.py:102
  101.1 1.5 convolution_bitcast_fusion
  102.6 0.0 reduce-scatter.5.cloned.1.call-done
  102.6 2.8 %bitcast_convert_fusion = f32[1,768,768]{2,1,0:T(8,128)} fusion(bf16[768,768]{1,0:T(8,128)(2,1)} %reduce-scatter.5.cloned.1.call-done), kind=kLoop, calls=%fused_computation.44 | loop fusion | flops 589824 | bytes 3538944 | tf_op jit(solution)/shard_map/broadcast_in_dim | solution.py:113
  105.5 52.0 %reduce-scatter.3.cloned.1.call-done = bf16[192,3072]{1,0:T(8,128)(2,1)} async-done(((bf16[768,3072]{1,0:T(8,128)(2,1)}), bf16[192,3072]{1,0:T(8,128)(2,1)}) %reduce-scatter.3.cloned.1.call-update) | async-done | bytes 1179664 | tf_op jit(solution)/shard_map/reduce_scatter | solution.py:64
  157.5 2.9 %bitcast_convert_fusion.1 = f32[1,192,3072]{2,1,0:T(8,128)} fusion(bf16[192,3072]{1,0:T(8,128)(2,1)} %reduce-scatter.3.cloned.1.call-done), kind=kLoop, calls=%fused_computation.45 | loop fusion | flops 589824 | bytes 3538944 | tf_op jit(solution)/shard_map/broadcast_in_dim | solution.py:113
  (17 shorter events, 0.2 us)
Async XLA Ops:
  7.2 2.8 %copy-start = (bf16[384,1,768]{2,0,1:T(8,128)(2,1)S(1)}, bf16[384,1,768]{2,0,1:T(8,128)(2,1)}, u32[]{:S(2)}) copy-start(bf16[384,1,768]{2,0,1:T(8,128)(2,1)} %param.8) | copy-start | bytes 1769476
  7.2 2.7 %copy-start.2 = (f32[1,768]{1,0:T(1,128)S(1)}, f32[1,768]{1,0:T(1,128)}, u32[]{:S(2)}) copy-start(f32[1,768]{1,0:T(1,128)} %param.12) | copy-start | bytes 9220
  7.2 2.7 %copy-start.3 = (f32[1,768]{1,0:T(1,128)S(1)}, f32[1,768]{1,0:T(1,128)}, u32[]{:S(2)}) copy-start(f32[1,768]{1,0:T(1,128)} %param.13) | copy-start | bytes 9220
  7.2 95.4 %reduce-scatter.5.cloned.1.call-start = ((), (), s32[]{:S(2)}) async-start(), calls=%async_computation.6 | async-start | bytes 5898240 | tf_op jit(solution)/shard_map/reduce_scatter | solution.py:67
  20.8 1.1 copy-start.1
  27.0 130.5 %reduce-scatter.3.cloned.1.call-start = ((), (), s32[]{:S(2)}) async-start(), calls=%async_computation.5 | async-start | bytes 5898240 | tf_op jit(solution)/shard_map/reduce_scatter | solution.py:64
  33.9 1.4 copy-start.6
  45.9 7.7 %copy-start.5 = (s32[1,384,1]{1,2,0:T(1,128)S(1)}, s32[1,384,1]{1,2,0:T(1,128)}, u32[]{:S(2)}) copy-start(s32[1,384,1]{1,2,0:T(1,128)} %param.14) | copy-start | bytes 4612
  45.9 9.4 %copy-start.4 = (s32[1,384]{1,0:T(1,128)S(1)}, s32[1,384]{1,0:T(1,128)}, u32[]{:S(2)}) copy-start(s32[1,384]{1,0:T(1,128)} %param.15) | copy-start | bytes 4612
  47.0 23.4 %all-to-all-start.1 = ((bf16[384,8,96]{0,2,1:T(8,128)(2,1)}), bf16[384,8,96]{0,2,1:T(8,128)(2,1)S(1)}, u32[]{:S(2)}, u32[]{:S(2)}) async-start(bf16[384,8,96]{0,2,1:T(8,128)(2,1)} %bitcast.8), calls=%async_computation.3 | async-start | bytes 1179648 | tf_op jit(solution)/shard_map/all_to_all | solution.py:74
  70.4 8.5 %all-to-all-start = ((bf16[4,1,240]{2,1,0:T(2,128)(2,1)}), bf16[4,1,240]{2,1,0:T(2,128)(2,1)S(1)}, u32[]{:S(2)}, u32[]{:S(2)}) async-start(bf16[4,1,240]{2,1,0:T(2,128)(2,1)} %convert_element_type.137), calls=%async_computation.2 | async-start | bytes 8192 | tf_op jit(solution)/shard_map/all_to_all | solution.py:103
  78.9 22.2 %all-to-all-start.2 = ((bf16[4,240,768]{2,1,0:T(8,128)(2,1)}), bf16[4,240,768]{2,1,0:T(8,128)(2,1)S(1)}, u32[]{:S(2)}, u32[]{:S(2)}) async-start(bf16[4,240,768]{2,1,0:T(8,128)(2,1)} %bitcast.10), calls=%async_computation.4 | async-start | bytes 2949120 | tf_op jit(solution)/shard_map/all_to_all | solution.py:102
Sparse Core Ops, SparseCore 0:
  27.1 68.5 reduce-scatter.4
  98.7 58.7 reduce-scatter.2
where the time goes:
time: 168 us; the launch traced here: 167 us
  waiting for transfers between devices  86.8 us (52%)
  matrix products  36.1 us (21%)
  between operations  14.2 us (8%)
  starting transfers between devices  14 us (8%)
  other arithmetic  11.5 us (7%)
  local copies, waits for them, and re-layouts  4.61 us (3%)
    reduce_scatter x1, waiting for transfers between devices, per_device(): lax.psum_scatter(up_whole.astype(jnp.bfloat16), 'dp', scatter_dimension=0...  52 us
    all_to_all x1, waiting for transfers between devices, per_device(): lax.all_to_all(send_grad, 'dp', split_axis=0, concat_axis=0, tiled=True)  18.5 us
    all_to_all x1, waiting for transfers between devices, per_device(): lax.all_to_all(grad_sum.reshape(batch_rows, pieces, width // pieces), 'to...  14 us
    dot_general x2, matrix products, contract_cols(): lax.dot_general(left, right, (((1,), (1,)), ((), ())), preferred_element_...  12.3 us
    dot_general x2, matrix products, contract_rows(): lax.dot_general(left, right, (((0,), (0,)), ((), ())), preferred_element_...  9.4 us
    all_to_all x1, starting transfers between devices, per_device(): lax.all_to_all(grad_sum.reshape(batch_rows, pieces, width // pieces), 'to...  6.64 us
    dot_general x1, matrix products, per_device(): pre_act = jnp.dot(hidden_in, w_up[0], preferred_element_type=jnp.float32)  6.38 us
    broadcast_in_dim x2, other arithmetic, per_device(): return (grad_up[None], grad_down[None], row_grad[None])  5.78 us
  transfers between devices with their start and end apart: 5, of which 4 were waited for; matrix products, arithmetic and copies ran while one was open for 17% of the time, Pallas kernels for 0%

commit v1 on v0

--- a/solution.py
+++ b/solution.py
@@ -71,12 +71,20 @@
     grad_hidden = contract_cols(grad_pre, w_up[0]) + grad_wide
     grad_sum = norm_back(grad_hidden * gain_first[0], normed, inv_scale).astype(jnp.bfloat16)
     pieces = lax.axis_size("token")
-    swapped = lax.all_to_all(
-        grad_sum.reshape(batch_rows, pieces, width // pieces),
-        "token",
-        split_axis=1,
-        concat_axis=1,
-        tiled=True,
+    swapped = jnp.concatenate(
+        lax.all_to_all(
+            jnp.stack(
+                jnp.split(
+                    grad_sum.reshape(batch_rows, pieces, width // pieces),
+                    lax.axis_size("token"),
+                    axis=1,
+                )
+            ),
+            "token",
+            0,
+            0,
+        ),
+        axis=1,
     )
     embed_grad = (
         grad_sum.astype(jnp.float32) + swapped.reshape(batch_rows, width).astype(jnp.float32)

time: 168 us -> 161 us (0.958)
  waiting for transfers between devices: 86.8 us -> 75.5 us
  local copies, waits for them, and re-layouts: 4.61 us -> 8.97 us
    reduce_scatter x1, waiting for transfers between devices: 52 us -> 34.7 us  [per_device(): lax.psum_scatter(up_whole.astype(jnp.bfloat16), 'dp', scatter_dimension=0...]
    all_to_all x1, waiting for transfers between devices: 18.5 us -> 24.5 us  [per_device(): lax.all_to_all(send_grad, 'dp', split_axis=0, concat_axis=0, tiled=True)]
    unnamed x14 -> x21, local copies, waits for them, and re-layouts: 2.21 us -> 6.69 us
  transfers between devices with their start and end apart: 5 -> 5, of which waited for: 4 -> 4; matrix products, arithmetic and copies ran while one was open for 17% -> 20% of each run, Pallas kernels for 0% -> 0%
where the time goes in v1:
time: 161 us; the launch traced here: 160 us
  waiting for transfers between devices  75.5 us (47%)
  matrix products  36.1 us (22%)
  between operations  14.2 us (9%)
  starting transfers between devices  14 us (9%)
  other arithmetic  11.4 us (7%)
  local copies, waits for them, and re-layouts  8.97 us (6%)
    reduce_scatter x1, waiting for transfers between devices, per_device(): lax.psum_scatter(up_whole.astype(jnp.bfloat16), 'dp', scatter_dimension=0...  34.7 us
    all_to_all x1, waiting for transfers between devices, per_device(): lax.all_to_all(send_grad, 'dp', split_axis=0, concat_axis=0, tiled=True)  24.5 us
    all_to_all x1, waiting for transfers between devices, per_device(): lax.all_to_all(jnp.stack(jnp.split(grad_sum.reshape(batch_rows, pieces, w...  14 us
    dot_general x2, matrix products, contract_cols(): lax.dot_general(left, right, (((1,), (1,)), ((), ())), preferred_element_...  12.3 us
    dot_general x2, matrix products, contract_rows(): lax.dot_general(left, right, (((0,), (0,)), ((), ())), preferred_element_...  9.4 us
    unnamed x21, local copies, waits for them, and re-layouts  6.69 us
    all_to_all x1, starting transfers between devices, per_device(): lax.all_to_all(jnp.stack(jnp.split(grad_sum.reshape(batch_rows, pieces, w...  6.64 us
    dot_general x1, matrix products, per_device(): pre_act = jnp.dot(hidden_in, w_up[0], preferred_element_type=jnp.float32)  6.38 us
  transfers between devices with their start and end apart: 5, of which 4 were waited for; matrix products, arithmetic and copies ran while one was open for 20% of the time, Pallas kernels for 0%

profile of v1, /device:TPU:0, one launch (start us, length us, event | category | flops | bytes accessed | tf_op | source)
XLA Modules:
  0.0 160.3 jit_solution(14971728084430291873)
XLA Ops:
  7.2 0.0 copy-start
  7.2 0.0 copy-start.2
  7.2 0.0 copy-start.3
  7.2 0.0 reduce-scatter.5.cloned.1.call-start
  7.2 1.3 convert_reduce_fusion
  8.5 1.4 fusion.36
  9.9 0.0 copy-done.2
  9.9 0.0 copy-done.3
  10.0 0.0 copy-done
  10.0 6.4 %multiply_convert_fusion = (bf16[384,3072]{1,0:T(8,128)(2,1)S(1)}, f32[384,3072]{1,0:T(8,128)}) fusion(bf16[1,768,3072]{2,1,0:T(8,128)(2,1)} %param.10, bf16[384,1,768]{2,0,1:T(8,128)(2,1)S(1)} %copy-done, f32[768]{0:T(1024)S(1)} %reduce.1, f32[384]{0:T(512)S(1)} %add_rsqrt_fusion.1, f32[384]{0:T(512)S(1)} %broadcast_multiply_fusion.5), kind=kOutput, calls=%fused_computation.17 | convolution fusion | flops 1819312128 | bytes 12392448 | tf_op jit(solution)/shard_map/dot_general | solution.py:48
  16.4 4.4 %fusion.72 = (f32[384]{0:T(512)S(1)}, f32[384,768]{1,0:T(8,128)S(1)}) fusion(f32[768]{0:T(1024)S(1)} %reduce.1, f32[384]{0:T(512)S(1)} %add_rsqrt_fusion.1, f32[384]{0:T(512)S(1)} %broadcast_multiply_fusion.5, bf16[384,1,768]{2,0,1:T(8,128)(2,1)S(1)} %copy-done, bf16[384,3072]{1,0:T(8,128)(2,1)S(1)} %get-tuple-element.7, bf16[1,3072,768]{2,1,0:T(8,128)(2,1)} %param.11), kind=kOutput, calls=%fused_computation.103 | convolution fusion | flops 1814298240 | bytes 8855040 | tf_op jit(solution)/shard_map/dot_general | solution.py:51
  20.8 0.0 copy-start.1
  20.8 0.3 multiply_reduce_fusion
  21.1 0.8 copy-done.1
  21.9 0.4 fusion.42
  22.3 4.7 %convolution_convert_fusion = bf16[3072,768]{1,0:T(8,128)(2,1)} fusion(bf16[384,3072]{1,0:T(8,128)(2,1)S(1)} %get-tuple-element.7, f32[384,768]{1,0:T(8,128)S(1)} %get-tuple-element.10, bf16[384,1,768]{2,0,1:T(8,128)(2,1)S(1)} %copy-done.1, f32[384]{0:T(512)S(1)} %get-tuple-element.12, f32[384]{0:T(512)S(1)} %get-tuple-element.13, f32[768]{0:T(1024)S(1)} %reduce.2, ...), kind=kOutput, calls=%fused_computation.1 | convolution fusion | flops 1816952832 | bytes 8856576 | tf_op jit(solution)/shard_map/dot_general | solution.py:31
  27.0 0.0 reduce-scatter.5.cloned.1.call-update
  27.0 0.0 reduce-scatter.3.cloned.1.call-start
  27.0 6.8 %fusion.5 = bf16[384,3072]{1,0:T(8,128)(2,1)S(1)} fusion(f32[384,3072]{1,0:T(8,128)} %get-tuple-element.8, bf16[1,3072,768]{2,1,0:T(8,128)(2,1)} %param.11, f32[384,768]{1,0:T(8,128)S(1)} %get-tuple-element.10, bf16[384,1,768]{2,0,1:T(8,128)(2,1)S(1)} %copy-done.1, f32[384]{0:T(512)S(1)} %get-tuple-element.12, f32[384]{0:T(512)S(1)} %get-tuple-element.13, ...), kind=kOutput, calls=%fused_computation.8 | convolution fusion | flops 1826390016 | bytes 13575168 | tf_op jit(solution)/shard_map/dot_general | solution.py:37
  33.9 0.0 copy-start.6
  33.9 1.4 copy-done.6
  35.3 4.7 %convolution_convert_fusion.1 = bf16[768,3072]{1,0:T(8,128)(2,1)} fusion(bf16[384,3072]{1,0:T(8,128)(2,1)S(1)} %fusion.5, bf16[384,1,768]{2,0,1:T(8,128)(2,1)S(1)} %copy-done, f32[768]{0:T(1024)S(1)} %reduce.1, f32[384]{0:T(512)S(1)} %add_rsqrt_fusion.1, f32[384]{0:T(512)S(1)} %broadcast_multiply_fusion.5), kind=kOutput, calls=%fused_computation.2 | convolution fusion | flops 1815773184 | bytes 7673856 | tf_op jit(solution)/shard_map/dot_general | solution.py:31
  40.0 0.0 reduce-scatter.3.cloned.1.call-update
  40.0 5.5 %fusion.71 = (f32[384]{0:T(512)S(1)}, f32[384]{0:T(512)S(1)}, f32[384,768]{1,0:T(8,128)S(1)}) fusion(f32[384]{0:T(512)S(1)} %add_rsqrt_fusion.1, f32[384]{0:T(512)S(1)} %broadcast_multiply_fusion.5, bf16[384,1,768]{2,0,1:T(8,128)(2,1)S(1)} %copy-done, f32[768]{0:T(1024)S(1)} %reduce.1, f32[384]{0:T(512)S(1)} %get-tuple-element.12, ...), kind=kOutput, calls=%fused_computation.102 | convolution fusion | flops 1816657152 | bytes 10635264 | tf_op jit(solution)/shard_map/dot_general | solution.py:37
  45.5 0.4 fusion.35
  45.9 0.3 copy.25
  46.2 0.0 copy-start.5
  46.2 0.0 copy-start.4
  46.2 0.6 fusion.64
  46.9 0.6 fusion.63
  47.5 0.6 fusion.62
  48.2 0.6 fusion.61
  48.8 0.6 fusion.60
  49.4 0.6 fusion.59
  50.1 0.6 fusion.58
  50.7 0.6 fusion.57
  51.4 6.6 %all-to-all-start.1 = ((bf16[8,384,1,96]{1,3,2,0:T(8,128)(2,1)}), bf16[8,384,1,96]{1,3,2,0:T(8,128)(2,1)S(1)}, u32[]{:S(2)}, u32[]{:S(2)}) async-start(bf16[8,384,1,96]{1,3,2,0:T(8,128)(2,1)} %fusion.57), calls=%async_computation.3 | async-start | bytes 1179648 | tf_op jit(solution)/shard_map/all_to_all | solution.py:75
  58.0 0.0 copy-done.5
  58.0 1.2 reduce-window.6
  59.3 0.2 slice_reduce_fusion
  59.5 0.2 reduce-window.9
  59.7 0.0 copy-done.4
  59.7 0.1 add_bitcast_fusion
  59.8 0.2 select_reduce_fusion
  60.0 0.7 convert_element_type.142
  60.7 14.0 %all-to-all-done.1 = bf16[8,384,1,96]{1,3,2,0:T(8,128)(2,1)S(1)} async-done(((bf16[8,384,1,96]{1,3,2,0:T(8,128)(2,1)}), bf16[8,384,1,96]{1,3,2,0:T(8,128)(2,1)S(1)}, u32[]{:S(2)}, u32[]{:S(2)}) %all-to-all-start.1) | async-done | bytes 589856 | tf_op jit(solution)/shard_map/all_to_all | solution.py:75
  74.7 3.7 %all-to-all-start = ((bf16[4,1,240]{2,1,0:T(2,128)(2,1)}), bf16[4,1,240]{2,1,0:T(2,128)(2,1)S(1)}, u32[]{:S(2)}, u32[]{:S(2)}) async-start(bf16[4,1,240]{2,1,0:T(2,128)(2,1)} %convert_element_type.142), calls=%async_computation.2 | async-start | bytes 8192 | tf_op jit(solution)/shard_map/all_to_all | solution.py:111
  78.4 0.1 convert_element_type.141
  78.5 0.4 copy.26
  78.9 2.1 %convolution_convert_fusion.2 = bf16[960,768]{1,0:T(8,128)(2,1)} fusion(s32[384]{0:T(512)S(1)} %multiply_add_fusion, f32[384,768]{1,0:T(8,128)S(1)} %copy.26, bf16[384,768]{1,0:T(8,128)(2,1)S(1)} %fusion.35), kind=kOutput, calls=%fused_computation.22 | convolution fusion | flops 568221696 | bytes 3245568 | tf_op jit(solution)/shard_map/dot_general | solution.py:103
  81.0 2.3 %all-to-all-done = bf16[4,1,240]{2,1,0:T(2,128)(2,1)S(1)} async-done(((bf16[4,1,240]{2,1,0:T(2,128)(2,1)}), bf16[4,1,240]{2,1,0:T(2,128)(2,1)S(1)}, u32[]{:S(2)}, u32[]{:S(2)}) %all-to-all-start) | async-done | bytes 1952 | tf_op jit(solution)/shard_map/all_to_all | solution.py:111
  83.3 3.6 %all-to-all-start.2 = ((bf16[4,240,768]{2,1,0:T(8,128)(2,1)}), bf16[4,240,768]{2,1,0:T(8,128)(2,1)S(1)}, u32[]{:S(2)}, u32[]{:S(2)}) async-start(bf16[4,240,768]{2,1,0:T(8,128)(2,1)} %bitcast.19), calls=%async_computation.4 | async-start | bytes 2949120 | tf_op jit(solution)/shard_map/all_to_all | solution.py:110
  86.9 0.1 reshape.147
  87.0 24.5 %all-to-all-done.2 = bf16[4,240,768]{2,1,0:T(8,128)(2,1)S(1)} async-done(((bf16[4,240,768]{2,1,0:T(8,128)(2,1)}), bf16[4,240,768]{2,1,0:T(8,128)(2,1)S(1)}, u32[]{:S(2)}, u32[]{:S(2)}) %all-to-all-start.2) | async-done | bytes 1474592 | tf_op jit(solution)/shard_map/all_to_all | solution.py:110
  111.5 1.5 convolution_bitcast_fusion
  113.0 0.0 reduce-scatter.5.cloned.1.call-done
  113.0 2.8 %bitcast_convert_fusion = f32[1,768,768]{2,1,0:T(8,128)} fusion(bf16[768,768]{1,0:T(8,128)(2,1)} %reduce-scatter.5.cloned.1.call-done), kind=kLoop, calls=%fused_computation.44 | loop fusion | flops 589824 | bytes 3538944 | tf_op jit(solution)/shard_map/broadcast_in_dim | solution.py:121
  115.8 34.7 %reduce-scatter.3.cloned.1.call-done = bf16[192,3072]{1,0:T(8,128)(2,1)} async-done(((bf16[768,3072]{1,0:T(8,128)(2,1)}), bf16[192,3072]{1,0:T(8,128)(2,1)}) %reduce-scatter.3.cloned.1.call-update) | async-done | bytes 1179664 | tf_op jit(solution)/shard_map/reduce_scatter | solution.py:64
  150.5 2.9 %bitcast_convert_fusion.1 = f32[1,192,3072]{2,1,0:T(8,128)} fusion(bf16[192,3072]{1,0:T(8,128)(2,1)} %reduce-scatter.3.cloned.1.call-done), kind=kLoop, calls=%fused_computation.45 | loop fusion | flops 589824 | bytes 3538944 | tf_op jit(solution)/shard_map/broadcast_in_dim | solution.py:121
  (17 shorter events, 0.2 us)
Async XLA Ops:
  7.2 2.8 %copy-start = (bf16[384,1,768]{2,0,1:T(8,128)(2,1)S(1)}, bf16[384,1,768]{2,0,1:T(8,128)(2,1)}, u32[]{:S(2)}) copy-start(bf16[384,1,768]{2,0,1:T(8,128)(2,1)} %param.8) | copy-start | bytes 1769476
  7.2 2.7 %copy-start.2 = (f32[1,768]{1,0:T(1,128)S(1)}, f32[1,768]{1,0:T(1,128)}, u32[]{:S(2)}) copy-start(f32[1,768]{1,0:T(1,128)} %param.12) | copy-start | bytes 9220
  7.2 2.7 %copy-start.3 = (f32[1,768]{1,0:T(1,128)S(1)}, f32[1,768]{1,0:T(1,128)}, u32[]{:S(2)}) copy-start(f32[1,768]{1,0:T(1,128)} %param.13) | copy-start | bytes 9220
  7.2 105.8 %reduce-scatter.5.cloned.1.call-start = ((), (), s32[]{:S(2)}) async-start(), calls=%async_computation.6 | async-start | bytes 5898240 | tf_op jit(solution)/shard_map/reduce_scatter | solution.py:67
  20.8 1.1 copy-start.1
  27.0 123.5 %reduce-scatter.3.cloned.1.call-start = ((), (), s32[]{:S(2)}) async-start(), calls=%async_computation.5 | async-start | bytes 5898240 | tf_op jit(solution)/shard_map/reduce_scatter | solution.py:64
  33.9 1.4 copy-start.6
  46.2 11.8 %copy-start.5 = (s32[1,384,1]{1,2,0:T(1,128)S(1)}, s32[1,384,1]{1,2,0:T(1,128)}, u32[]{:S(2)}) copy-start(s32[1,384,1]{1,2,0:T(1,128)} %param.14) | copy-start | bytes 4612
  46.2 13.4 %copy-start.4 = (s32[1,384]{1,0:T(1,128)S(1)}, s32[1,384]{1,0:T(1,128)}, u32[]{:S(2)}) copy-start(s32[1,384]{1,0:T(1,128)} %param.15) | copy-start | bytes 4612
  51.4 23.4 %all-to-all-start.1 = ((bf16[8,384,1,96]{1,3,2,0:T(8,128)(2,1)}), bf16[8,384,1,96]{1,3,2,0:T(8,128)(2,1)S(1)}, u32[]{:S(2)}, u32[]{:S(2)}) async-start(bf16[8,384,1,96]{1,3,2,0:T(8,128)(2,1)} %fusion.57), calls=%async_computation.3 | async-start | bytes 1179648 | tf_op jit(solution)/shard_map/all_to_all | solution.py:75
  74.7 8.5 %all-to-all-start = ((bf16[4,1,240]{2,1,0:T(2,128)(2,1)}), bf16[4,1,240]{2,1,0:T(2,128)(2,1)S(1)}, u32[]{:S(2)}, u32[]{:S(2)}) async-start(bf16[4,1,240]{2,1,0:T(2,128)(2,1)} %convert_element_type.142), calls=%async_computation.2 | async-start | bytes 8192 | tf_op jit(solution)/shard_map/all_to_all | solution.py:111
  83.3 28.2 %all-to-all-start.2 = ((bf16[4,240,768]{2,1,0:T(8,128)(2,1)}), bf16[4,240,768]{2,1,0:T(8,128)(2,1)S(1)}, u32[]{:S(2)}, u32[]{:S(2)}) async-start(bf16[4,240,768]{2,1,0:T(8,128)(2,1)} %bitcast.19), calls=%async_computation.4 | async-start | bytes 2949120 | tf_op jit(solution)/shard_map/all_to_all | solution.py:110
Sparse Core Ops, SparseCore 0:
  27.1 59.7 reduce-scatter.4
  89.9 60.5 reduce-scatter.2
